TPU v7x, 256 devices: a whole 4x4x8 slice. The times are simulated.
256 devices in a mesh: grp: 8 (over x, y_hi), feat: 32 (over y_lo, z, core).
Axes of the slice: x: 4, y: 4 (y_hi: 2, y_lo: 2; y = y_hi * 2 + y_lo), z: 8, core: 2. Of those that a mesh axis runs over, the one named last changes fastest.
Arguments:
- resid: bfloat16 [4, 512, 2304], P(None, 'grp'), may hold values from -6 to 6
- w_enc: bfloat16 [4, 2304, 8192], P(None, None, 'feat'), may hold values from -0.125 to 0.125
- b_enc: float32 [4, 8192], P(None, 'feat'), may hold values from -3 to 3
- w_dec: bfloat16 [4, 8, 8192, 2304], P(None, 'grp', 'feat'), may hold values from -0.0625 to 0.0625
- targets: bfloat16 [8, 512, 2304], P('grp'), may hold values from -6 to 6
- start_layer: int32 [4, 32], P(None, 'feat'), may hold values from 0 to 7, as said below
Outputs:
- active: bfloat16 [512, 4, 8192], P('grp', None, 'feat')
- recon: bfloat16 [8, 512, 2304], P('grp', 'feat')
- recon_loss: float32 [], replicated
- feat_grad: float32 [512, 4, 8192], P('grp', None, 'feat')
Inputs may be any that keep to these rules, and one draw needn't show every extreme that they name: `start_layer`: each column is nondecreasing over source layers; in every column the first source feeds from target 0 and the last source feeds only target 8 - 1.
All inputs are finite; a program needn't handle non-finite values.
Results may differ from a plain program's by a relative error of at most 0.0049.
Values may be sent and summed in bfloat16 or wider, within the bound.
A program may use at most 64 MiB of HBM per device.

v0:
```python
from functools import partial

import jax
import jax.numpy as jnp
from jax import lax
from jax.sharding import PartitionSpec as P


def per_device(resid, w_enc, b_enc, w_dec, targets, start_layer):
    sources = resid.shape[0]
    targets_here = w_dec.shape[1]
    model_width = resid.shape[2]
    block_width = w_dec.shape[2]
    group_index = lax.axis_index("grp")
    target_ids = group_index * targets_here + jnp.arange(targets_here, dtype=jnp.int32)
    feeds_mask = target_ids[None, :] >= start_layer[:, 0][:, None]
    feeds_value = feeds_mask.astype(jnp.float32)

    def masked(source, target, product):
        return feeds_value[source, target] * product()

    encoded = []
    for source in range(sources):
        pre_act = (
            jnp.dot(resid[source], w_enc[source], preferred_element_type=jnp.float32)
            + b_enc[source]
        )
        encoded.append(jnp.maximum(pre_act, 0.0).astype(jnp.bfloat16))
    active = jnp.stack(encoded, axis=1)
    piece_rows = lax.all_gather(active, "grp", axis=0, tiled=True)
    row_count = piece_rows.shape[0]
    target = 0
    summed = jnp.zeros((row_count, model_width), jnp.float32)
    for source in range(sources):
        product = partial(
            jnp.dot,
            piece_rows[:, source],
            w_dec[source, target],
            preferred_element_type=jnp.float32,
        )
        summed = summed + masked(source, target, product)
    outputs = [summed]
    partial_sums = jnp.stack(outputs, axis=0)
    tokens = partial_sums.shape[1]
    rows_feat = tokens // lax.axis_size("feat")
    my_first = lax.axis_index("feat") * rows_feat
    recon_rows = lax.psum_scatter(partial_sums, "feat", scatter_dimension=1, tiled=True)
    own_targets = lax.dynamic_slice_in_dim(targets, my_first, rows_feat, 1)
    difference = recon_rows - own_targets.astype(jnp.float32)
    error_all = lax.all_gather(difference.astype(jnp.bfloat16), "feat", axis=1, tiled=True)
    squares = jnp.sum(difference * difference)
    entries = targets_here * lax.axis_size("grp") * tokens * model_width
    recon_loss = lax.psum(squares, ("grp", "feat")) / entries
    row_count = active.shape[0] * lax.axis_size("grp")
    error_block = lax.slice_in_dim(error_all, 0, row_count, axis=1)
    gradients = []
    for source in range(sources):
        summed = jnp.zeros((row_count, block_width), jnp.float32)
        target = 0
        product = partial(
            lax.dot_general,
            error_block[target],
            w_dec[source, target],
            (((1,), (1,)), ((), ())),
            preferred_element_type=jnp.float32,
        )
        summed = summed + masked(source, target, product)
        gradients.append(summed)
    feat_grad = lax.psum_scatter(
        jnp.stack(gradients, axis=1), "grp", scatter_dimension=0, tiled=True
    )
    return (active, recon_rows.astype(jnp.bfloat16), recon_loss, feat_grad)


def solution(mesh):
    in_specs = (
        P(None, "grp", None),
        P(None, None, "feat"),
        P(None, "feat"),
        P(None, "grp", "feat", None),
        P("grp", None, None),
        P(None, "feat"),
    )
    out_specs = (P("grp", None, "feat"), P("grp", "feat", None), P(), P("grp", None, "feat"))
    return jax.shard_map(
        per_device, mesh=mesh, in_specs=in_specs, out_specs=out_specs, check_vma=False
    )
```

profile of v0, /device:TPU:2, one launch (start us, length us, event | category | flops | bytes accessed | tf_op | source)
XLA Modules:
  0.0 372.0 jit_solution(16647181485218019645)
XLA Ops:
  7.2 0.0 copy-start.3
  7.2 0.0 all-gather.3.cloned.1.call-start
  7.2 0.8 fusion.121
  8.1 1.7 fusion.95
  9.8 1.7 fusion.92
  11.5 0.0 copy-start.4
  11.5 0.0 copy-done.3
  11.5 1.6 fusion.101
  13.1 1.6 fusion.98
  14.7 0.0 slice-start
  14.8 0.7 pad_maximum_fusion.1
  15.4 0.0 all-gather.3.cloned.1.call-update
  15.5 0.0 reduce-scatter.3.cloned.1.call-start
  15.5 0.0 copy-done.4
  15.5 0.6 fusion.122
  16.2 54.4 %all-gather.3.cloned.1.call-done = bf16[512,4,256]{2,0,1:T(8,128)(2,1)} async-done(((bf16[64,4,256]{2,0,1:T(8,128)(2,1)}), bf16[512,4,256]{2,0,1:T(8,128)(2,1)}) %all-gather.3.cloned.1.call-update) | async-done | bytes 1048592 | tf_op jit(solution)/shard_map/all_gather | solution.py:30
  70.6 0.0 slice-start.1
  70.6 0.0 copy-start
  70.6 3.3 convolution_multiply_fusion.3
  73.9 0.0 slice-done
  73.9 0.0 slice-done.1
  73.9 0.0 copy-done
  74.0 1.4 fusion.2
  75.4 1.4 fusion.1
  76.9 3.6 fusion.3
  80.5 0.0 reduce-scatter.3.cloned.1.call-update
  80.5 0.0 all-gather.5.cloned.1.call-start
  80.5 123.8 %reduce-scatter.3.cloned.1.call-done = f32[1,16,2304]{2,1,0:T(8,128)} async-done(((f32[1,512,2304]{2,1,0:T(8,128)}), f32[1,16,2304]{2,1,0:T(8,128)}) %reduce-scatter.3.cloned.1.call-update) | async-done | bytes 147472 | tf_op jit(solution)/shard_map/reduce_scatter | solution.py:47
  204.3 2.3 fusion.120
  206.6 0.0 all-gather.5.cloned.1.call-update
  206.6 0.0 reduce-scatter.5.cloned.1.call-start
  206.7 60.8 %all-gather.5.cloned.1.call-done = bf16[1,512,2304]{2,1,0:T(8,128)(2,1)} async-done(((bf16[1,16,2304]{2,1,0:T(8,128)(2,1)}), bf16[1,512,2304]{2,1,0:T(8,128)(2,1)}) %all-gather.5.cloned.1.call-update) | async-done | bytes 2359312 | tf_op jit(solution)/shard_map/all_gather | solution.py:50
  267.5 0.0 copy-start.2
  267.5 3.6 fusion.21
  271.1 0.0 copy-done.2
  271.1 2.7 fusion.27
  273.8 2.7 fusion.33
  276.5 2.7 fusion.15
  279.2 0.0 copy-start.1
  279.3 1.5 pad_maximum_fusion
  280.8 0.0 reduce-scatter.5.cloned.1.call-update
  280.8 0.0 copy-done.1
  280.8 0.8 copy.10
  281.5 77.1 %psum.7 = f32[]{:T(128)} all-reduce(f32[]{:T(128)} %get-tuple-element.9), channel_id=1, replica_groups=mesh['grp'=8,'feat'=32] {'grp','feat'}, use_global_device_ids=true, to_apply=%region_2.0 | all-reduce | flops 1 | bytes 8 | tf_op jit(solution)/shard_map/psum | solution.py:53
  359.3 3.2 reduce-scatter.5.cloned.1.call-done
  362.5 1.8 copy.11
  (2 shorter events, 0.0 us)
Async XLA Ops:
  7.2 4.3 %copy-start.3 = (bf16[4,64,2304]{2,1,0:T(8,128)(2,1)S(1)}, bf16[4,64,2304]{2,1,0:T(8,128)(2,1)}, u32[]{:S(2)}) copy-start(bf16[4,64,2304]{2,1,0:T(8,128)(2,1)} %param.6) | copy-start | bytes 3538948
  7.2 63.4 %all-gather.3.cloned.1.call-start = ((), (), s32[]{:S(2)}) async-start(), calls=%async_computation.2 | async-start | bytes 1179648 | tf_op jit(solution)/shard_map/all_gather | solution.py:30
  11.5 4.0 %copy-start.4 = (s32[4,1]{0,1:T(1,128)S(1)}, s32[4,1]{0,1:T(1,128)}, u32[]{:S(2)}) copy-start(s32[4,1]{0,1:T(1,128)} %param.11) | copy-start | bytes 52
  14.7 59.2 %slice-start = ((s8[4718592]{0:T(1024)(128)(4,1)}), s8[524288]{0:T(1024)(128)(4,1)S(1)}, s32[]{:S(2)}) async-start(s8[4718592]{0:T(1024)(128)(4,1)} %bitcast.139), calls=%async_computation.6 | async-start | bytes 1048576
  15.5 188.8 %reduce-scatter.3.cloned.1.call-start = ((), (), s32[]{:S(2)}) async-start(), calls=%async_computation.3 | async-start | bytes 4866048 | tf_op jit(solution)/shard_map/reduce_scatter | solution.py:47
  70.6 3.3 slice-start.1
  70.6 3.3 copy-start
  80.5 187.0 %all-gather.5.cloned.1.call-start = ((), (), s32[]{:S(2)}) async-start(), calls=%async_computation.4 | async-start | bytes 2433024 | tf_op jit(solution)/shard_map/all_gather | solution.py:50
  206.6 155.8 %reduce-scatter.5.cloned.1.call-start = ((), (), s32[]{:S(2)}) async-start(), calls=%async_computation.5 | async-start | bytes 2359296 | tf_op jit(solution)/shard_map/reduce_scatter | solution.py:69
  267.5 3.6 copy-start.2
  279.2 1.5 copy-start.1
Sparse Core Ops, SparseCore 0:
  15.6 54.9 all-gather.2
  80.6 123.6 reduce-scatter.2
  206.8 60.6 all-gather.4
  280.9 81.5 reduce-scatter.4
where the time goes:
time: 372 us
  waiting for transfers between devices  242 us (65%)
  blocking collectives  77.1 us (21%)
  matrix products  28.1 us (8%)
  between operations  15.7 us (4%)
  other arithmetic  4.49 us (1%)
  local copies, waits for them, and re-layouts  4.1 us (1%)
    reduce_scatter x1, waiting for transfers between devices, per_device(): lax.psum_scatter(partial_sums, 'feat', scatter_dimension=1, tiled=True)  124 us
    psum x1, blocking collectives, per_device(): recon_loss = lax.psum(squares, ('grp', 'feat')) / entries  77.1 us
    all_gather x1, waiting for transfers between devices, per_device(): lax.all_gather(difference.astype(jnp.bfloat16), 'feat', axis=1, tiled=True)  60.8 us
    all_gather x1, waiting for transfers between devices, per_device(): piece_rows = lax.all_gather(active, 'grp', axis=0, tiled=True)  54.4 us
    dot_general x8, matrix products, masked(): return feeds_value[source, target] * product()  21.5 us
  transfers between devices with their start and end apart: 4, of which 4 were waited for; matrix products, arithmetic and copies ran while one was open for 0% of the time, Pallas kernels for 0%

commit v1 on v0

v1 whole, which is shorter than its diff:
```python
import jax
import jax.numpy as jnp
from jax import lax
from jax.experimental import pallas as pl
from jax.experimental.pallas import tpu as pltpu
from jax.sharding import PartitionSpec as P

MESH = pl.DeviceIdType.MESH
BF = jnp.bfloat16
F32 = jnp.float32

NX, NZ = 4, 8
GRP, FEAT = 8, 32
SRC, TOKENS, WIDTH, BLOCK = 4, 512, 2304, 256
OWN = TOKENS // GRP
ROWS = TOKENS // FEAT
ALL_K = SRC * BLOCK
CUT = 1024
CA, CB = slice(0, CUT), slice(CUT, WIDTH)
WA, WB = CUT, WIDTH - CUT
TILE = 256
N_SEMS = 256


class Net:
    def __init__(self, send_sems, recv_sems):
        self.send_sems, self.recv_sems = send_sems, recv_sems
        self.copies = {}

    def send(self, key, src, dst, device):
        n = len(self.copies)
        copy = pltpu.make_async_remote_copy(
            src_ref=src,
            dst_ref=dst,
            send_sem=self.send_sems.at[n],
            recv_sem=self.recv_sems.at[n],
            device_id=device,
            device_id_type=MESH,
        )
        self.copies[key] = copy
        copy.start()

    def arrived(self, key):
        self.copies[key].wait_recv()

    def finish(self):
        for copy in self.copies.values():
            copy.wait_send()


def kernel(
    resid, w_enc, b_enc, w_dec, targets, start,
    act_out, recon_out, loss_out, grad_out,
    resid_v, wenc_v, wdec_v, targ_v, act_all, lhs, part, x_out, x_in, y_out, y_in,
    za_out, za_in, zb_out, zb_in, ya_out, ya_in, own, err, grads,
    r_out, r_in, q_out, q_in, ry_out, ry_in, lz, lc, lg, vsum,
    load_sems, send_sems, recv_sems,
):
    g, f = lax.axis_index("grp"), lax.axis_index("feat")
    x, yh = lax.div(g, 2), lax.rem(g, 2)
    c = lax.rem(f, 2)
    z = lax.rem(lax.div(f, 2), NZ)
    yl = lax.div(f, 2 * NZ)

    def feat_of(yl_, z_, c_):
        return (yl_ * NZ + z_) * 2 + c_

    def zat(d):
        return lax.rem(z + d + NZ, NZ)

    def xat(d):
        return lax.rem(x + d + NX, NX)

    partner = (g, feat_of(yl, z, 1 - c))
    yside = (g, feat_of(1 - yl, z, c))
    zside = {d: (g, feat_of(yl, zat(d), c)) for d in (1, -1)}
    gpair = (x * 2 + 1 - yh, f)
    xside = {d: (xat(d) * 2 + yh, f) for d in (1, -1)}
    spot = yl * 2 + c

    def flip(a, m, bits):
        out = 0
        for b in range(bits):
            bit = lax.rem(lax.div(a, 1 << b), 2)
            out = out + ((1 - bit) if (m >> b) & 1 else bit) * (1 << b)
        return out

    zpeers = {d: (g, feat_of(yl, zat(d), c)) for d in range(1, NZ)}

    def spot_peer(m):
        s = flip(spot, m, 2)
        return (g, feat_of(lax.div(s, 2), z, lax.rem(s, 2)))

    spots = {m: spot_peer(m) for m in range(1, 4)}
    gpeers = {m: (flip(g, m, 3), f) for m in range(1, GRP)}

    barrier = pltpu.get_barrier_semaphore()
    peers = [*zpeers.values(), *spots.values(), *gpeers.values()]
    for peer in peers:
        pl.semaphore_signal(barrier, inc=1, device_id=peer, device_id_type=MESH)

    loads = []

    def load(src, dst):
        copy = pltpu.make_async_copy(src, dst, load_sems.at[len(loads)])
        loads.append(copy)
        copy.start()
        return copy

    enc_loads = [(load(resid.at[s], resid_v.at[s]), load(w_enc.at[s], wenc_v.at[s])) for s in range(SRC)]
    dec_loads = [load(w_dec.at[s, 0], wdec_v.at[pl.ds(s * BLOCK, BLOCK)]) for s in range(SRC)]
    targ_load = load(targets.at[0, pl.ds(f * ROWS, ROWS)], targ_v)

    net = Net(send_sems, recv_sems)
    feeds = [jnp.where(g >= start[s, 0], 1.0, 0.0).astype(F32) for s in range(SRC)]

    def act_at(group, s, half=None):
        first = group * 2 if half is None else group * 2 + half
        return act_all.at[pl.ds(first, 2 if half is None else 1), :, :, pl.ds(s * BLOCK, BLOCK)]

    for s in range(SRC):
        for copy in enc_loads[s]:
            copy.wait()
        pre = jnp.dot(resid_v[s], wenc_v[s], preferred_element_type=F32) + b_enc[pl.ds(s, 1), :]
        a = jnp.maximum(pre, 0.0).astype(BF)
        act_out[s] = a
        act_all[pl.ds(g * 2, 2), :, :, pl.ds(s * BLOCK, BLOCK)] = a.reshape(2, 2, ROWS, BLOCK)
        if s == 0:
            pl.semaphore_wait(barrier, len(peers))
        mine = act_at(g, s)
        net.send(("a", s), mine, mine, gpair)
        for d in (1, -1):
            net.send(("x", s, d), mine, mine, xside[d])
    other = x * 2 + 1 - yh
    for s in range(SRC):
        net.arrived(("a", s))
        block = act_at(other, s)
        for d in (1, -1):
            net.send(("xy", s, d), block, block, xside[d])
    for kind, row in (("x", yh), ("xy", 1 - yh)):
        for s in range(SRC):
            for half, d in ((0, 1), (1, -1)):
                net.arrived((kind, s, d))
                block = act_at(xat(-d) * 2 + row, s, half)
                net.send((kind + "f", s, d), block, block, xside[d])
    for kind in ("xf", "xyf"):
        for s in range(SRC):
            for d in (1, -1):
                net.arrived((kind, s, d))

    for copy in dec_loads:
        copy.wait()
    feed_row = jnp.concatenate([jnp.full((1, BLOCK), feeds[s], F32) for s in range(SRC)], axis=1)

    @pl.loop(0, 2 * NZ)
    def _(i):
        for h in range(2):
            lhs[h, i] = (act_all[i, h].astype(F32) * feed_row).astype(BF)

    def decode(core, first, tiles, out):
        @pl.loop(0, tiles)
        def _(n):
            cols = pl.ds(pl.multiple_of(first + n * TILE, TILE), TILE)
            a = lhs[core].reshape(2 * NZ * ROWS, ALL_K)
            p = jnp.dot(a, wdec_v[:, cols], preferred_element_type=F32)
            out[:, :, cols] = p.reshape(2 * NZ, ROWS, TILE).astype(out.dtype)

    decode(1 - c, CUT, WB // TILE, x_out)
    net.send("pB", x_out.at[:, :, CB], x_in.at[:, :, CB], partner)
    decode(1 - c, 0, WA // TILE, x_out)
    net.send("pA", x_out.at[:, :, CA], x_in.at[:, :, CA], partner)
    decode(c, CUT, WB // TILE, part)

    def chip(row, cols):
        return part[row, :, cols] + x_in[row, :, cols].astype(F32)

    z_order = (4, -3, 3, -2, 2, -1, 1, 0)
    net.arrived("pB")
    for i, d in enumerate(z_order):
        y_out[i] = chip((1 - yl) * NZ + zat(d), CB).astype(BF)
        net.send(("y", d), y_out.at[i], y_in.at[i], yside)
    decode(c, 0, WA // TILE, part)
    net.arrived("pA")

    first_way = {0: -1, 1: 1, 2: -1}

    def own_sum(stream, d):
        if stream == 0:
            return chip((1 - yl) * NZ + zat(d), CA)
        if stream == 1:
            return chip(yl * NZ + zat(d), CA)
        i = z_order.index(d if d > -4 else 4)
        net.arrived(("y", z_order[i]))
        return chip(yl * NZ + zat(d), CB) + y_in[i].astype(F32)

    def ring_in(stream, way, k):
        net.arrived(("z", stream, way, k))
        i = 0 if way < 0 else 1
        return (zb_in[i, k] if stream == 2 else za_in[stream, i, k]).astype(F32)

    def hop(stream, k):
        for way in (-1, 1):
            if k == 0 and way != first_way[stream]:
                continue
            value = own_sum(stream, way * (4 - k))
            if k > 1 or (k == 1 and way == first_way[stream]):
                value = value + ring_in(stream, way, k - 1)
            i = 0 if way < 0 else 1
            out, into = (zb_out, zb_in) if stream == 2 else (za_out.at[stream], za_in.at[stream])
            out[i, k] = value.astype(BF)
            net.send(("z", stream, way, k), out.at[i, k], into.at[i, k], zside[way])

    def last(stream):
        return own_sum(stream, 0) + ring_in(stream, -1, 3) + ring_in(stream, 1, 3)

    targ_load.wait()
    hop(0, 0)
    hop(1, 0)
    hop(2, 0)
    for k in (1, 2, 3):
        for stream in (0, 1, 2):
            hop(stream, k)
    ya_out[...] = last(0).astype(BF)
    net.send("ya", ya_out, ya_in, yside)
    own[...] = last(1)

    def close(value, cols):
        recon_out[:, cols] = value.astype(BF)
        diff = value - targ_v[:, cols].astype(F32)
        err[c, yl, z, :, cols] = diff.astype(BF)
        square = diff * diff
        total = square[:, 0:128]
        for i in range(1, square.shape[1] // 128):
            total = total + square[:, i * 128 : (i + 1) * 128]
        return total[0:8] + total[8:16]

    def err_at(y, d, cols=None):
        z_ = zat(d)
        return err.at[c, y, z_] if cols is None else err.at[c, y, z_, :, cols]

    loss = close(last(2), CB)
    far = {0: -1, 1: 1, 2: -1}

    def spread(stream, way, k):
        y, cols = ((yl, CA), (1 - yl, CA), (yl, CB))[stream]
        if k < 3 or (k == 3 and way == far[stream]):
            block = err_at(y, -way * k, cols)
            net.send(("e", stream, way, k + 1), block, block, zside[way])

    for way in (-1, 1):
        spread(2, way, 0)
    block = err_at(yl, 0, CB)
    net.send(("eyB", 0, 0), block, block, yside)
    net.arrived("ya")
    loss = loss + close(own[...] + ya_in[...].astype(F32), CA)
    block = err_at(yl, 0, CA)
    net.send("eyA", block, block, yside)
    for way in (-1, 1):
        spread(0, way, 0)
    block = err_at(yl, 0)
    net.send(("p0", 0, 0), block, block, partner)

    lz[z] = loss
    for d in range(1, NZ):
        net.send(("lz", d), lz.at[z], lz.at[z], zpeers[d])

    net.arrived("eyA")
    for way in (-1, 1):
        spread(1, way, 0)

    def total_of(slots, n):
        total = slots[0]
        for i in range(1, n):
            total = total + slots[i]
        return total

    def to_partner_y(way, k):
        net.arrived(("eyB", way, k))
        block = err_at(1 - yl, -way * k)
        net.send(("p1", way, k), block, block, partner)

    def gradient(steps):
        ds = [-way * k if way else k for way, k in steps]
        for way, k in steps:
            net.arrived(("p0", way, k))
            net.arrived(("p1", way, k))
        rows = jnp.concatenate([err[:, :, zat(d)].reshape(4 * ROWS, WIDTH) for d in ds], axis=0)
        for s in range(SRC):
            p = lax.dot_general(
                rows, wdec_v[pl.ds(s * BLOCK, BLOCK), :], (((1,), (1,)), ((), ())), preferred_element_type=F32
            )
            p = p * feeds[s]
            for j, d in enumerate(ds):
                for core in range(2):
                    for y in range(2):
                        r = (j * 4 + core * 2 + y) * ROWS
                        grads[y * NZ + zat(d), core, :, pl.ds(s * BLOCK, BLOCK)] = p[r : r + ROWS]

    steps_of = {k: [(-1, k), (1, k)] for k in (1, 2, 3)}
    steps_of[0] = [(0, 0)]
    steps_of[4] = [(0, 4)]

    to_partner_y(0, 0)
    for k in (1, 2, 3):
        for way in (-1, 1):
            net.arrived(("e", 2, way, k))
            spread(2, way, k)
            block = err_at(yl, -way * k, CB)
            net.send(("eyB", way, k), block, block, yside)
        for way in (-1, 1):
            net.arrived(("e", 0, way, k))
            spread(0, way, k)
            block = err_at(yl, -way * k)
            net.send(("p0", way, k), block, block, partner)
        for way in (-1, 1):
            net.arrived(("e", 1, way, k))
            spread(1, way, k)
        gradient(steps_of[k - 1])
        if k == 1:
            for d in range(1, NZ):
                net.arrived(("lz", d))
            lc[spot] = total_of(lz, NZ)
            for m in spots:
                net.send(("lc", m), lc.at[spot], lc.at[spot], spots[m])
        if k == 2:
            for m in spots:
                net.arrived(("lc", m))
            lg[g] = total_of(lc, 4)
            for m in gpeers:
                net.send(("lg", m), lg.at[g], lg.at[g], gpeers[m])
        for way in (-1, 1):
            to_partner_y(way, k)
    net.arrived(("e", 2, far[2], 4))
    block = err_at(yl, 4, CB)
    net.send(("eyB", 0, 4), block, block, yside)
    net.arrived(("e", 0, far[0], 4))
    block = err_at(yl, 4)
    net.send(("p0", 0, 4), block, block, partner)
    net.arrived(("e", 1, far[1], 4))
    gradient(steps_of[3])
    net.arrived(("eyB", 0, 4))
    block = err_at(1 - yl, 4)
    net.send(("p1", 0, 4), block, block, partner)
    for m in gpeers:
        net.arrived(("lg", m))
    loss_out[0, 0] = jnp.sum(total_of(lg, GRP)) / (GRP * TOKENS * WIDTH)
    gradient(steps_of[4])

    def grad_at(xd, pair, s):
        row = 1 - yh if pair else yh
        return grads[pl.ds((xat(xd) * 2 + row) * 2, 2), :, :, pl.ds(s * BLOCK, BLOCK)].reshape(OWN, BLOCK)

    ways = {-1: True, 1: False}
    for s in range(SRC):
        for way in (-1, 1):
            i = 0 if way < 0 else 1
            r_out[s, i, 0] = grad_at(2, ways[way], s).astype(BF)
            net.send(("r", s, way, 0), r_out.at[s, i, 0], r_in.at[s, i, 0], xside[way])
        for way in (-1, 1):
            i = 0 if way < 0 else 1
            q_out[s, i] = grad_at(way, not ways[way], s).astype(BF)
            net.send(("q", s, way), q_out.at[s, i], q_in.at[s, i], xside[way])
    for s in range(SRC):
        for way in (-1, 1):
            i = 0 if way < 0 else 1
            net.arrived(("r", s, way, 0))
            r_out[s, i, 1] = (grad_at(way, ways[way], s) + r_in[s, i, 0].astype(F32)).astype(BF)
            net.send(("r", s, way, 1), r_out.at[s, i, 1], r_in.at[s, i, 1], xside[way])
    for s in range(SRC):
        net.arrived(("q", s, 1))
        net.arrived(("q", s, -1))
        net.arrived(("r", s, -1, 1))
        u = grad_at(0, True, s) + r_in[s, 0, 1].astype(F32) + q_in[s, 1].astype(F32)
        ry_out[s] = u.astype(BF)
        net.send(("ry", s), ry_out.at[s], ry_in.at[s], gpair)
        net.arrived(("r", s, 1, 1))
        vsum[s] = grad_at(0, False, s) + r_in[s, 1, 1].astype(F32) + q_in[s, 0].astype(F32)
    for s in range(SRC):
        net.arrived(("ry", s))
        grad_out[s] = vsum[s] + ry_in[s].astype(F32)
    net.finish()


def per_device(resid, w_enc, b_enc, w_dec, targets, start_layer):
    vmem = pl.BlockSpec(memory_space=pltpu.VMEM)
    smem = pl.BlockSpec(memory_space=pltpu.SMEM)
    anywhere = pl.BlockSpec(memory_space=pl.ANY)
    blocks = 2 * NZ
    act, recon, loss, grad = pl.pallas_call(
        kernel,
        out_shape=(
            jax.ShapeDtypeStruct((SRC, OWN, BLOCK), BF),
            jax.ShapeDtypeStruct((ROWS, WIDTH), BF),
            jax.ShapeDtypeStruct((1, 1), F32),
            jax.ShapeDtypeStruct((SRC, OWN, BLOCK), F32),
        ),
        in_specs=[anywhere, anywhere, vmem, anywhere, anywhere, smem],
        out_specs=(vmem, vmem, smem, vmem),
        scratch_shapes=[
            pltpu.VMEM((SRC, OWN, WIDTH), BF),
            pltpu.VMEM((SRC, WIDTH, BLOCK), BF),
            pltpu.VMEM((ALL_K, WIDTH), BF),
            pltpu.VMEM((ROWS, WIDTH), BF),
            pltpu.VMEM((blocks, 2, ROWS, ALL_K), BF),
            pltpu.VMEM((2, blocks, ROWS, ALL_K), BF),
            pltpu.VMEM((blocks, ROWS, WIDTH), F32),
            pltpu.VMEM((blocks, ROWS, WIDTH), BF),
            pltpu.VMEM((blocks, ROWS, WIDTH), BF),
            pltpu.VMEM((NZ, ROWS, WB), BF),
            pltpu.VMEM((NZ, ROWS, WB), BF),
            pltpu.VMEM((2, 2, 4, ROWS, WA), BF),
            pltpu.VMEM((2, 2, 4, ROWS, WA), BF),
            pltpu.VMEM((2, 4, ROWS, WB), BF),
            pltpu.VMEM((2, 4, ROWS, WB), BF),
            pltpu.VMEM((ROWS, WA), BF),
            pltpu.VMEM((ROWS, WA), BF),
            pltpu.VMEM((ROWS, WA), F32),
            pltpu.VMEM((2, 2, NZ, ROWS, WIDTH), BF),
            pltpu.VMEM((blocks, 2, ROWS, ALL_K), F32),
            pltpu.VMEM((SRC, 2, 2, OWN, BLOCK), BF),
            pltpu.VMEM((SRC, 2, 2, OWN, BLOCK), BF),
            pltpu.VMEM((SRC, 2, OWN, BLOCK), BF),
            pltpu.VMEM((SRC, 2, OWN, BLOCK), BF),
            pltpu.VMEM((SRC, OWN, BLOCK), BF),
            pltpu.VMEM((SRC, OWN, BLOCK), BF),
            pltpu.VMEM((NZ, 8, 128), F32),
            pltpu.VMEM((4, 8, 128), F32),
            pltpu.VMEM((GRP, 8, 128), F32),
            pltpu.VMEM((SRC, OWN, BLOCK), F32),
            pltpu.SemaphoreType.DMA((16,)),
            pltpu.SemaphoreType.DMA((N_SEMS,)),
            pltpu.SemaphoreType.DMA((N_SEMS,)),
        ],
        compiler_params=pltpu.CompilerParams(
            collective_id=0, has_side_effects=True, vmem_limit_bytes=60 * 1024 * 1024
        ),
    )(resid, w_enc, b_enc, w_dec, targets, start_layer)
    return (
        act.transpose(1, 0, 2),
        recon[None],
        loss[0, 0],
        grad.transpose(1, 0, 2),
    )


def solution(mesh):
    in_specs = (
        P(None, "grp", None),
        P(None, None, "feat"),
        P(None, "feat"),
        P(None, "grp", "feat", None),
        P("grp", None, None),
        P(None, "feat"),
    )
    out_specs = (P("grp", None, "feat"), P("grp", "feat", None), P(), P("grp", None, "feat"))
    return jax.shard_map(
        per_device, mesh=mesh, in_specs=in_specs, out_specs=out_specs, check_vma=False
    )
```

time: 372 us -> 96.6 us (0.26)
  waiting for transfers between devices: 242 us -> 0 us
  Pallas kernels: 0 us -> 86.1 us
  blocking collectives: 77.1 us -> 0 us
  matrix products: 28.1 us -> 0 us
  between operations: 15.7 us -> 2.4 us
  other arithmetic: 4.49 us -> 0 us
    reduce_scatter x2 -> x0, waiting for transfers between devices: 127 us -> none  [the longest x1 124 us: per_device(): lax.psum_scatter(partial_sums, 'feat', scatter_dimension=1, tiled=True)]
    all_gather x2 -> x0, waiting for transfers between devices: 115 us -> none  [the longest x1 60.8 us: per_device(): lax.all_gather(difference.astype(jnp.bfloat16), 'feat', axis=1, tiled=True)]
    pallas_call x0 -> x1, Pallas kernels: none -> 86.1 us  [per_device(): pl.pallas_call(kernel, out_shape=(jax.ShapeDtypeStruct((SRC, OWN, BLOCK),...]
    psum x1 -> x0, blocking collectives: 77.1 us -> none  [per_device(): recon_loss = lax.psum(squares, ('grp', 'feat')) / entries]
    dot_general x12 -> x0, matrix products: 28.1 us -> none  [the longest x8 21.5 us: masked(): return feeds_value[source, target] * product()]
  transfers between devices with their start and end apart: 4 -> 0, of which waited for: 4 -> 0; matrix products, arithmetic and copies ran while one was open for 0% -> 0% of each run, Pallas kernels for 0% -> 0%
where the time goes in v1:
time: 96.6 us; the launch traced here: 94.9 us
  Pallas kernels  86.1 us (89%)
  local copies, waits for them, and re-layouts  6.32 us (7%)
  between operations  2.4 us (2%)
    pallas_call x1, Pallas kernels, per_device(): pl.pallas_call(kernel, out_shape=(jax.ShapeDtypeStruct((SRC, OWN, BLOCK),...  86.1 us
    unnamed x4, local copies, waits for them, and re-layouts  6.32 us

profile of v1, /device:TPU:2, one launch (start us, length us, event | category | flops | bytes accessed | tf_op | source)
XLA Modules:
  0.0 94.9 jit_solution(5357077452620790133)
XLA Ops:
  0.6 1.3 %copy.10.start = s32[4,1]{1,0:T(4,128)} copy(s32[4,1]{0,1:T(1,128)} %param.11) | data formatting | bytes 32 | tf_op args[5]
  1.9 86.1 %shard_map.93 = (bf16[4,64,256]{2,1,0:T(8,128)(2,1)}, bf16[16,2304]{1,0:T(8,128)(2,1)}, f32[1,1]{1,0:T(1,128)}, f32[4,64,256]{2,1,0:T(8,128)}) custom-call(bf16[4,64,2304]{2,1,0:T(8,128)(2,1)} %resid.1, bf16[4,2304,256]{2,1,0:T(8,128)(2,1)} %w_enc.1, f32[4,256]{1,0:T(4,128)} %b_enc.1, bf16[4,1,256,2304]{3,2,1,0:T(8,128)(2,1)} %w_dec.1, ...), custom_call_target="tpu_custom_call" | custom-call | tf_op jit(solution)/shard_map/pallas_call | solution.py:389
  88.1 1.7 %copy.11 = bf16[64,4,256]{2,1,0:T(4,128)(2,1)} copy(bf16[64,4,256]{2,0,1:T(8,128)(2,1)} %bitcast.5) | data formatting | bytes 262144
  89.7 1.8 %copy.12 = f32[64,4,256]{2,1,0:T(4,128)} copy(f32[64,4,256]{2,0,1:T(8,128)} %bitcast.4) | data formatting | bytes 524288
  91.6 1.5 %copy.15 = bf16[1,16,2304]{2,1,0:T(8,128)(2,1)} copy(bf16[1,16,2304]{2,1,0:T(8,128)(2,1)} %bitcast.6) | data formatting | bytes 147456
